TPU v7x, 32 devices: a whole 2x2x4 slice. The times are simulated.
32 devices in a mesh: dp: 8 (over y, x, core), fsdp: 4 (over z).
Axes of the slice: x: 2, y: 2, z: 4, core: 2. Of those that a mesh axis runs over, the one named last changes fastest.
Arguments:
- tokens: bfloat16 [32768, 768], P(('dp', 'fsdp')), may hold values from -8 to 8
- chip_ids: int32 [32768], P(('dp', 'fsdp')), may hold values from 0 to 511, as said below
- ln1_gain: bfloat16 [768], P('fsdp'), may hold values from 0.5 to 1.5
- ln1_bias: bfloat16 [768], P('fsdp'), may hold values from -1.5 to 1.5
- w_qkv: bfloat16 [768, 2304], P('fsdp'), may hold values from -0.3125 to 0.3125
- w_out: bfloat16 [768, 768], P('fsdp'), may hold values from -0.625 to 0.625
- b_out: bfloat16 [768], P('fsdp'), may hold values from -1.5 to 1.5
- ln2_gain: bfloat16 [768], P('fsdp'), may hold values from 0.5 to 1.5
- ln2_bias: bfloat16 [768], P('fsdp'), may hold values from -1.5 to 1.5
- w_fc1: bfloat16 [768, 3072], P('fsdp'), may hold values from -0.21875 to 0.21875
- b_fc1: bfloat16 [3072], P('fsdp'), may hold values from -2.5 to 2.5
- w_fc2: bfloat16 [3072, 768], P('fsdp'), may hold values from -0.15625 to 0.15625
- b_fc2: bfloat16 [768], P('fsdp'), may hold values from -1.5 to 1.5
- cotangent: bfloat16 [32768, 768], P(('dp', 'fsdp')), may hold values from -6 to 6
Outputs:
- layer_out: bfloat16 [32768, 768], P(('dp', 'fsdp'))
- grad_tokens: float32 [32768, 768], P(('dp', 'fsdp'))
- grad_ln1_gain: float32 [768], P('fsdp')
- grad_ln1_bias: float32 [768], P('fsdp')
- grad_w_qkv: float32 [768, 2304], P('fsdp')
- grad_w_out: float32 [768, 768], P('fsdp')
- grad_b_out: float32 [768], P('fsdp')
- grad_ln2_gain: float32 [768], P('fsdp')
- grad_ln2_bias: float32 [768], P('fsdp')
- grad_w_fc1: float32 [768, 3072], P('fsdp')
- grad_b_fc1: float32 [3072], P('fsdp')
- grad_w_fc2: float32 [3072, 768], P('fsdp')
- grad_b_fc2: float32 [768], P('fsdp')
Inputs may be any that keep to these rules, and one draw needn't show every extreme that they name: `chip_ids`: chip numbers never fall along the tokens. Each chip holds exactly 64 or 256 tokens and lies inside one device's block of 1024 rows; every such block holds at least one chip of 256 tokens and may hold only such chips. The chips of the d-th block of rows carry numbers from d * 16 to (d + 1) * 16 - 1, the first and the last of them always used.
All inputs are finite; a program needn't handle non-finite values.
Results may differ from a plain program's by a relative error of at most 0.015.
Values may be sent and summed in bfloat16 or wider, within the bound.
No kernel may reach another device: no remote copies, remote signals or barrier semaphores. Data moves between devices by JAX's collectives and lax.ppermute only.
A program may use at most 320 MiB of HBM per device.

v0:
```python
import math
import jax
import jax.numpy as jnp
from jax import lax
from jax.sharding import PartitionSpec as P

HEADS = 12
epsilon = 1e-05
neg_big = -1e30
inv_sqrt_two = 1.0 / math.sqrt(2.0)
inv_sqrt_tau = 1.0 / math.sqrt(2.0 * math.pi)


def layer_norm(token_rows, gain_vec, shift_vec):
    centred = token_rows - jnp.mean(token_rows, axis=-1, keepdims=True)
    inverse = lax.rsqrt(jnp.mean(centred * centred, axis=-1, keepdims=True) + epsilon)
    normed = centred * inverse
    return (normed * gain_vec + shift_vec, normed, inverse)


def norm_back(grad_rows, normed, inverse, gain_vec):
    d_gain = jnp.sum(grad_rows * normed, axis=0)
    d_shift = jnp.sum(grad_rows, axis=0)
    inner_grad = grad_rows * gain_vec
    d_rows = inverse * (
        inner_grad
        - jnp.mean(inner_grad, axis=-1, keepdims=True)
        - normed * jnp.mean(inner_grad * normed, axis=-1, keepdims=True)
    )
    return (d_rows, d_gain, d_shift)


def weight_grad(left_side, right_side):
    return lax.dot_general(
        left_side, right_side, (((0,), (0,)), ((), ())), preferred_element_type=jnp.float32
    )


def input_grad(grad_side, weight):
    return lax.dot_general(
        grad_side, weight, (((1,), (1,)), ((), ())), preferred_element_type=jnp.float32
    )


def head_major(qkv_all):
    length = qkv_all.shape[0]
    head_size = qkv_all.shape[1] // (3 * HEADS)
    stacked = qkv_all.reshape(length, 3, HEADS, head_size).transpose(1, 2, 0, 3)
    return (stacked[0], stacked[1], stacked[2], 1.0 / math.sqrt(head_size))


def block_scores(query_block, key_heads, chip_block, chip_ids, scale_factor):
    scores = (
        jnp.einsum("hqe,hke->hqk", query_block, key_heads, preferred_element_type=jnp.float32)
        * scale_factor
    )
    same_chip = chip_block[:, None] == chip_ids[None, :]
    return jnp.where(same_chip[None], scores, neg_big)


def attend(qkv_all, chip_ids):
    queries, key_heads, value_heads, scale_factor = head_major(qkv_all)
    length = qkv_all.shape[0]
    block = min(512, length)
    mixed_parts = []
    sum_parts = []
    for start in range(0, length, block):
        scores = block_scores(
            queries[:, start : start + block],
            key_heads,
            chip_ids[start : start + block],
            chip_ids,
            scale_factor,
        )
        row_max = jnp.max(scores, axis=-1, keepdims=True)
        exp_score = jnp.exp(scores - row_max)
        row_total = jnp.sum(exp_score, axis=-1, keepdims=True)
        probs_low = (exp_score / row_total).astype(jnp.bfloat16)
        mixed_parts.append(
            jnp.einsum("hqk,hke->hqe", probs_low, value_heads, preferred_element_type=jnp.float32)
        )
        sum_parts.append(row_max + jnp.log(row_total))
    mixed = jnp.concatenate(mixed_parts, axis=1)
    return (mixed.transpose(1, 0, 2).reshape(length, -1), sum_parts)


def attend_back(qkv_all, chip_ids, sum_parts, grad_low):
    queries, key_heads, value_heads, scale_factor = head_major(qkv_all)
    length = qkv_all.shape[0]
    head_size = queries.shape[2]
    grad_heads = grad_low.reshape(length, HEADS, head_size).transpose(1, 0, 2)
    block = min(512, length)
    d_keys = jnp.zeros(key_heads.shape, jnp.float32)
    d_values = jnp.zeros(value_heads.shape, jnp.float32)
    query_parts = []
    for number, start in enumerate(range(0, length, block)):
        query_block = queries[:, start : start + block]
        grad_block = grad_heads[:, start : start + block]
        scores = block_scores(
            query_block, key_heads, chip_ids[start : start + block], chip_ids, scale_factor
        )
        attn_probs = jnp.exp(scores - sum_parts[number])
        probs_low = attn_probs.astype(jnp.bfloat16)
        d_values = d_values + jnp.einsum(
            "hqk,hqe->hke", probs_low, grad_block, preferred_element_type=jnp.float32
        )
        d_probs = jnp.einsum(
            "hqe,hke->hqk", grad_block, value_heads, preferred_element_type=jnp.float32
        )
        d_score = (
            attn_probs * (d_probs - jnp.sum(d_probs * attn_probs, axis=-1, keepdims=True))
        ).astype(jnp.bfloat16)
        query_parts.append(
            jnp.einsum("hqk,hke->hqe", d_score, key_heads, preferred_element_type=jnp.float32)
            * scale_factor
        )
        d_keys = (
            d_keys
            + jnp.einsum("hqk,hqe->hke", d_score, query_block, preferred_element_type=jnp.float32)
            * scale_factor
        )
    d_query = jnp.concatenate(query_parts, axis=1)
    combined = (
        jnp.stack([d_query, d_keys, d_values], axis=0).transpose(2, 0, 1, 3).reshape(length, -1)
    )
    return combined.astype(jnp.bfloat16)


def on_device(
    tokens,
    chip_ids,
    ln1_gain,
    ln1_bias,
    w_qkv,
    w_out,
    b_out,
    ln2_gain,
    ln2_bias,
    w_fc1,
    b_fc1,
    w_fc2,
    b_fc2,
    cotangent,
):
    gathered = (
        lax.all_gather(ln1_gain, "fsdp", axis=0, tiled=True),
        lax.all_gather(ln1_bias, "fsdp", axis=0, tiled=True),
        lax.all_gather(w_qkv, "fsdp", axis=0, tiled=True),
        lax.all_gather(w_out, "fsdp", axis=0, tiled=True),
        lax.all_gather(b_out, "fsdp", axis=0, tiled=True),
        lax.all_gather(ln2_gain, "fsdp", axis=0, tiled=True),
        lax.all_gather(ln2_bias, "fsdp", axis=0, tiled=True),
        lax.all_gather(w_fc1, "fsdp", axis=0, tiled=True),
        lax.all_gather(b_fc1, "fsdp", axis=0, tiled=True),
        lax.all_gather(w_fc2, "fsdp", axis=0, tiled=True),
        lax.all_gather(b_fc2, "fsdp", axis=0, tiled=True),
    )
    gain_one = gathered[0].astype(jnp.float32)
    gain_two = gathered[5].astype(jnp.float32)
    as_float = tokens.astype(jnp.float32)
    normed_in_f, normed_one, inverse_one = layer_norm(
        as_float, gain_one, gathered[1].astype(jnp.float32)
    )
    normed_in = normed_in_f.astype(jnp.bfloat16)
    qkv_all = jnp.dot(normed_in, gathered[2], preferred_element_type=jnp.float32).astype(
        jnp.bfloat16
    )
    attn_mixed, sum_parts = attend(qkv_all, chip_ids)
    mixed_low = attn_mixed.astype(jnp.bfloat16)
    hidden_one = as_float + (
        jnp.dot(mixed_low, gathered[3], preferred_element_type=jnp.float32)
        + gathered[4].astype(jnp.float32)
    )
    normed_mid_f, normed_two, inverse_two = layer_norm(
        hidden_one, gain_two, gathered[6].astype(jnp.float32)
    )
    normed_mid = normed_mid_f.astype(jnp.bfloat16)
    pre_act = jnp.dot(normed_mid, gathered[7], preferred_element_type=jnp.float32) + gathered[
        8
    ].astype(jnp.float32)
    activated = jax.nn.gelu(pre_act, approximate=False).astype(jnp.bfloat16)
    output = hidden_one + (
        jnp.dot(activated, gathered[9], preferred_element_type=jnp.float32)
        + gathered[10].astype(jnp.float32)
    )
    gathered = (
        lax.all_gather(ln1_gain, "fsdp", axis=0, tiled=True),
        lax.all_gather(ln1_bias, "fsdp", axis=0, tiled=True),
        lax.all_gather(w_qkv, "fsdp", axis=0, tiled=True),
        lax.all_gather(w_out, "fsdp", axis=0, tiled=True),
        lax.all_gather(b_out, "fsdp", axis=0, tiled=True),
        lax.all_gather(ln2_gain, "fsdp", axis=0, tiled=True),
        lax.all_gather(ln2_bias, "fsdp", axis=0, tiled=True),
        lax.all_gather(w_fc1, "fsdp", axis=0, tiled=True),
        lax.all_gather(b_fc1, "fsdp", axis=0, tiled=True),
        lax.all_gather(w_fc2, "fsdp", axis=0, tiled=True),
        lax.all_gather(b_fc2, "fsdp", axis=0, tiled=True),
    )
    grad_out = cotangent.astype(jnp.float32)
    d_b_fc2 = jnp.sum(cotangent.astype(jnp.float32), axis=0)
    d_w_fc2 = weight_grad(activated, cotangent)
    d_act = input_grad(cotangent, gathered[9])
    slope = (
        0.5 * (1.0 + jax.scipy.special.erf(pre_act * inv_sqrt_two))
        + pre_act * jnp.exp(-0.5 * pre_act * pre_act) * inv_sqrt_tau
    )
    d_pre_low = (d_act * slope).astype(jnp.bfloat16)
    d_b_fc1 = jnp.sum(d_pre_low.astype(jnp.float32), axis=0)
    d_w_fc1 = weight_grad(normed_mid, d_pre_low)
    d_mid = input_grad(d_pre_low, gathered[7])
    d_hidden_norm, d_ln2_gain, d_ln2_bias = norm_back(d_mid, normed_two, inverse_two, gain_two)
    d_hidden = grad_out + d_hidden_norm
    d_hidden_low = d_hidden.astype(jnp.bfloat16)
    d_b_out = jnp.sum(d_hidden_low.astype(jnp.float32), axis=0)
    d_w_out = weight_grad(mixed_low, d_hidden_low)
    d_mixed = input_grad(d_hidden_low, gathered[3]).astype(jnp.bfloat16)
    d_qkv = attend_back(qkv_all, chip_ids, sum_parts, d_mixed)
    d_w_qkv = weight_grad(normed_in, d_qkv)
    d_in = input_grad(d_qkv, gathered[2])
    d_in_norm, d_ln1_gain, d_ln1_bias = norm_back(d_in, normed_one, inverse_one, gain_one)
    d_tokens = d_hidden + d_in_norm
    all_rows = (
        lax.psum_scatter(
            d_ln1_gain.astype(jnp.bfloat16), "fsdp", scatter_dimension=0, tiled=True
        ).astype(jnp.float32),
        lax.psum_scatter(
            d_ln1_bias.astype(jnp.bfloat16), "fsdp", scatter_dimension=0, tiled=True
        ).astype(jnp.float32),
        lax.psum_scatter(
            d_w_qkv.astype(jnp.bfloat16), "fsdp", scatter_dimension=0, tiled=True
        ).astype(jnp.float32),
        lax.psum_scatter(
            d_w_out.astype(jnp.bfloat16), "fsdp", scatter_dimension=0, tiled=True
        ).astype(jnp.float32),
        lax.psum_scatter(
            d_b_out.astype(jnp.bfloat16), "fsdp", scatter_dimension=0, tiled=True
        ).astype(jnp.float32),
        lax.psum_scatter(
            d_ln2_gain.astype(jnp.bfloat16), "fsdp", scatter_dimension=0, tiled=True
        ).astype(jnp.float32),
        lax.psum_scatter(
            d_ln2_bias.astype(jnp.bfloat16), "fsdp", scatter_dimension=0, tiled=True
        ).astype(jnp.float32),
        lax.psum_scatter(
            d_w_fc1.astype(jnp.bfloat16), "fsdp", scatter_dimension=0, tiled=True
        ).astype(jnp.float32),
        lax.psum_scatter(
            d_b_fc1.astype(jnp.bfloat16), "fsdp", scatter_dimension=0, tiled=True
        ).astype(jnp.float32),
        lax.psum_scatter(
            d_w_fc2.astype(jnp.bfloat16), "fsdp", scatter_dimension=0, tiled=True
        ).astype(jnp.float32),
        lax.psum_scatter(
            d_b_fc2.astype(jnp.bfloat16), "fsdp", scatter_dimension=0, tiled=True
        ).astype(jnp.float32),
    )
    final_grads = tuple(
        lax.psum(
            (
                all_rows[0],
                all_rows[1],
                all_rows[2],
                all_rows[3],
                all_rows[4],
                all_rows[5],
                all_rows[6],
                all_rows[7],
                all_rows[8],
                all_rows[9],
                all_rows[10],
            ),
            "dp",
        )
    )
    return (output.astype(jnp.bfloat16), d_tokens) + final_grads


def solution(mesh):
    placed = (
        P(("dp", "fsdp"), None),
        P(("dp", "fsdp")),
        P("fsdp"),
        P("fsdp"),
        P("fsdp", None),
        P("fsdp", None),
        P("fsdp"),
        P("fsdp"),
        P("fsdp"),
        P("fsdp", None),
        P("fsdp"),
        P("fsdp", None),
        P("fsdp"),
        P(("dp", "fsdp"), None),
    )
    return jax.shard_map(
        on_device,
        mesh=mesh,
        in_specs=placed,
        out_specs=(
            P(("dp", "fsdp"), None),
            P(("dp", "fsdp"), None),
            P("fsdp"),
            P("fsdp"),
            P("fsdp", None),
            P("fsdp", None),
            P("fsdp"),
            P("fsdp"),
            P("fsdp"),
            P("fsdp", None),
            P("fsdp"),
            P("fsdp", None),
            P("fsdp"),
        ),
        check_vma=False,
    )
```

profile of v0, /device:TPU:0, one launch (start us, length us, event | category | flops | bytes accessed | tf_op | source)
XLA Modules:
  0.0 876.6 jit_solution(12832730221961627232)
XLA Ops:
  16.2 21.8 %all-reduce.15 = (bf16[768]{0:T(1024)(128)(2,1)S(1)}, bf16[768]{0:T(1024)(128)(2,1)S(1)}, bf16[768]{0:T(1024)(128)(2,1)S(1)}, bf16[768]{0:T(1024)(128)(2,1)S(1)}, bf16[768]{0:T(1024)(128)(2,1)S(1)}) all-reduce(bf16[768]{0:T(1024)(128)(2,1)S(1)} %dynamic-update-slice.1, ...), channel_id=1, replica_groups=mesh['dp'=8,'fsdp'=4] {'fsdp'}, use_global_device_ids=true, to_apply=%add.1 | all-reduce | flops 3840 | bytes 15360
  41.8 14.0 %all-gather = bf16[4,1,768]{2,1,0:T(2,128)(2,1)S(1)} all-gather(bf16[1,1,768]{2,1,0:T(2,128)(2,1)S(1)} %reshape.178), channel_id=1, replica_groups=mesh['dp'=8,'fsdp'=4] {'fsdp'}, dimensions={0}, use_global_device_ids=true | all-gather | bytes 7680 | tf_op jit(solution)/shard_map/all_gather | solution.py:154
  58.7 24.1 %all-gather.6.cloned.1.call-done = bf16[768,2304]{1,0:T(8,128)(2,1)} async-done(((bf16[192,2304]{1,0:T(8,128)(2,1)}), bf16[768,2304]{1,0:T(8,128)(2,1)}) %all-gather.6.cloned.1.call-update) | async-done | bytes 3538960 | tf_op jit(solution)/shard_map/all_gather | solution.py:148
  82.8 7.8 convolution_convert_fusion
  98.9 12.6 %fusion.28 = (f32[12,512]{1,0:T(8,128)S(1)}, f32[12,512,1024]{2,1,0:T(8,128)}) fusion(pred[512,1024]{1,0:T(8,128)(4,1)S(1)} %get-tuple-element.84, bf16[3,12,1024,64]{2,3,1,0:T(8,128)(2,1)} %bitcast.66, bf16[12,1024,64]{1,2,0:T(8,128)(2,1)S(1)} %slice_bitcast_fusion.2), kind=kOutput, calls=%fused_computation.48 | convolution fusion | flops 824174592 | bytes 28073984 | tf_op jit(solution)/shard_map/hqe,hke->hqk/dot_general | solution.py:54
  111.5 12.9 %fusion = f32[12,512]{1,0:T(8,128)S(1)} fusion(f32[12,512]{1,0:T(8,128)S(1)} %get-tuple-element.92, f32[12,512,1024]{2,1,0:T(8,128)} %get-tuple-element.93, pred[512,1024]{1,0:T(8,128)(4,1)S(1)} %get-tuple-element.84), kind=kLoop, calls=%fused_computation.12 | loop fusion | flops 25159680 | bytes 25739264 | tf_op jit(solution)/shard_map/reduce_sum | solution.py:77
  128.1 9.9 %fusion.51 = bf16[12,512,64]{1,2,0:T(8,128)(2,1)} fusion(f32[12,512]{1,0:T(8,128)S(1)} %fusion, f32[12,512]{1,0:T(8,128)S(1)} %get-tuple-element.92, f32[12,512,1024]{2,1,0:T(8,128)S(1)} %copy-done, pred[512,1024]{1,0:T(8,128)(4,1)S(1)} %get-tuple-element.84, bf16[3,12,1024,64]{2,3,1,0:T(8,128)(2,1)} %bitcast.67), kind=kOutput, calls=%fused_computation.95 | convolution fusion | flops 837156864 | bytes 28098560 | tf_op jit(solution)/shard_map/hqk,hke->hqe/dot_general | solution.py:80
  138.7 12.6 %fusion.29 = (f32[12,512]{1,0:T(8,128)S(1)}, f32[12,512,1024]{2,1,0:T(8,128)}) fusion(pred[512,1024]{1,0:T(8,128)(4,1)S(1)} %get-tuple-element.85, bf16[3,12,1024,64]{2,3,1,0:T(8,128)(2,1)} %bitcast.68, bf16[12,1024,64]{1,2,0:T(8,128)(2,1)S(1)} %slice_bitcast_fusion.2), kind=kOutput, calls=%fused_computation.49 | convolution fusion | flops 824174592 | bytes 28073984 | tf_op jit(solution)/shard_map/hqe,hke->hqk/dot_general | solution.py:54
  151.3 12.4 %fusion.1 = f32[12,512]{1,0:T(8,128)S(1)} fusion(f32[12,512]{1,0:T(8,128)S(1)} %get-tuple-element.90, f32[12,512,1024]{2,1,0:T(8,128)} %get-tuple-element.91, pred[512,1024]{1,0:T(8,128)(4,1)S(1)} %get-tuple-element.85), kind=kLoop, calls=%fused_computation.13 | loop fusion | flops 25159680 | bytes 25739264 | tf_op jit(solution)/shard_map/reduce_sum | solution.py:77
  166.8 9.3 %fusion.50 = bf16[12,512,64]{1,2,0:T(8,128)(2,1)S(1)} fusion(f32[12,512]{1,0:T(8,128)S(1)} %fusion.1, f32[12,512]{1,0:T(8,128)S(1)} %get-tuple-element.90, f32[12,512,1024]{2,1,0:T(8,128)S(1)} %copy-done.1, pred[512,1024]{1,0:T(8,128)(4,1)S(1)} %get-tuple-element.85, bf16[3,12,1024,64]{2,3,1,0:T(8,128)(2,1)} %bitcast.69), kind=kOutput, calls=%fused_computation.94 | convolution fusion | flops 837156864 | bytes 28098560 | tf_op jit(solution)/shard_map/hqk,hke->hqe/dot_general | solution.py:80
  181.9 21.5 %all-gather.10.cloned.1.call-done = bf16[768,3072]{1,0:T(8,128)(2,1)} async-done(((bf16[192,3072]{1,0:T(8,128)(2,1)}), bf16[768,3072]{1,0:T(8,128)(2,1)}) %all-gather.10.cloned.1.call-update) | async-done | bytes 4718608 | tf_op jit(solution)/shard_map/all_gather | solution.py:153
  203.4 39.0 %fusion.6 = (bf16[1024,3072]{1,0:T(8,128)(2,1)}, f32[1024,3072]{1,0:T(8,128)}) fusion(f32[3072]{0:T(1024)S(1)} %bitcast.82, bf16[768,3072]{1,0:T(8,128)(2,1)} %all-gather.10.cloned.1.call-done, f32[1024,768]{0,1:T(8,128)} %copy-done.4, f32[768]{0:T(1024)S(1)} %copy-done.43, f32[768]{0:T(1024)S(1)} %copy-done.35, f32[1024]{0:T(1024)S(1)} %add_rsqrt_fusion, ...), kind=kOutput, calls=%fused_computation.20 | convolution fusion | flops 5043388416 | bytes 26765312 | tf_op jit(solution)/shard_map/dot_general | solution.py:178
  242.4 50.3 %all-gather.12.cloned.1.call-done = bf16[3072,768]{1,0:T(8,128)(2,1)} async-done(((bf16[768,768]{1,0:T(8,128)(2,1)}), bf16[3072,768]{1,0:T(8,128)(2,1)}) %all-gather.12.cloned.1.call-update) | async-done | bytes 4718608 | tf_op jit(solution)/shard_map/all_gather | solution.py:155
  292.7 12.5 %fusion.83 = (bf16[3072]{0:T(1024)(128)(2,1)}, bf16[1024,3072]{1,0:T(8,128)(2,1)S(1)}) fusion(f32[1024,3072]{1,0:T(8,128)} %get-tuple-element.97, f32[3072]{0:T(1024)S(1)} %bitcast.83, bf16[1024,768]{1,0:T(8,128)(2,1)S(1)} %copy-done.18, bf16[3072,768]{1,0:T(8,128)(2,1)} %all-gather.12.cloned.1.call-done), kind=kOutput, calls=%fused_computation.145 | convolution fusion | flops 4869583872 | bytes 25184256 | tf_op jit(solution)/shard_map/dot_general | solution.py:40
  305.2 7.3 fusion.82
  323.4 20.8 %multiply_reduce_fusion = (f32[12,512]{1,0:T(8,128)S(1)}, f32[12,512,1024]{2,1,0:T(8,128)}) fusion(f32[12,512]{1,0:T(8,128)S(1)} %log_add_fusion, f32[12,512,1024]{2,1,0:T(8,128)} %get-tuple-element.91, pred[512,1024]{1,0:T(8,128)(4,1)S(1)} %copy-done.14, bf16[3,12,1024,64]{2,3,1,0:T(8,128)(2,1)} %bitcast.70, bf16[12,1024,64]{1,2,0:T(8,128)(2,1)S(1)} %bitcast.78), kind=kOutput, calls=%fused_computation.1 | convolution fusion | flops 836757504 | bytes 53272576 | tf_op jit(solution)/shard_map/hqe,hke->hqk/dot_general | solution.py:107
  344.2 13.4 %fusion.13 = f32[12,1024,64]{1,2,0:T(8,128)} fusion(f32[12,512]{1,0:T(8,128)S(1)} %log_add_fusion, f32[12,512,1024]{2,1,0:T(8,128)} %get-tuple-element.91, pred[512,1024]{1,0:T(8,128)(4,1)S(1)} %copy-done.14, bf16[12,1024,64]{1,2,0:T(8,128)(2,1)S(1)} %bitcast.79), kind=kOutput, calls=%fused_computation.27 | convolution fusion | flops 830472192 | bytes 29655040 | tf_op jit(solution)/shard_map/hqk,hqe->hke/dot_general | solution.py:104
  360.1 18.1 %multiply_reduce_fusion.1 = (f32[12,512]{1,0:T(8,128)S(1)}, f32[12,512,1024]{2,1,0:T(8,128)}) fusion(f32[12,512]{1,0:T(8,128)S(1)} %copy-done.28, f32[12,512,1024]{2,1,0:T(8,128)} %get-tuple-element.93, pred[512,1024]{1,0:T(8,128)(4,1)S(1)} %copy-done.12, bf16[3,12,1024,64]{2,3,1,0:T(8,128)(2,1)} %bitcast.71, bf16[12,1024,64]{1,2,0:T(8,128)(2,1)} %bitcast.80), kind=kOutput, calls=%fused_computation.4 | convolution fusion | flops 836757504 | bytes 53264384 | tf_op jit(solution)/shard_map/hqe,hke->hqk/dot_general | solution.py:107
  378.2 41.8 %multiply_convert_fusion = (bf16[12,512,1024]{2,1,0:T(8,128)(2,1)}, bf16[12,512,1024]{2,1,0:T(8,128)(2,1)}) fusion(f32[12,512,1024]{2,1,0:T(8,128)} %get-tuple-element.101, f32[12,512]{1,0:T(8,128)S(1)} %get-tuple-element.100, f32[12,512]{1,0:T(8,128)S(1)} %log_add_fusion, f32[12,512,1024]{2,1,0:T(8,128)} %get-tuple-element.91, ...), kind=kLoop, calls=%fused_computation | loop fusion | flops 75497472 | bytes 126976000 | tf_op jit(solution)/shard_map/convert_element_type | solution.py:112
  420.0 8.9 %multiply_convert_fusion.4 = bf16[12,512,64]{1,2,0:T(8,128)(2,1)S(1)} fusion(bf16[12,512,1024]{2,1,0:T(8,128)(2,1)} %get-tuple-element.109, bf16[3,12,1024,64]{2,3,1,0:T(8,128)(2,1)} %bitcast.72), kind=kOutput, calls=%fused_computation.90 | convolution fusion | flops 806092800 | bytes 14942208 | tf_op jit(solution)/shard_map/hqk,hke->hqe/dot_general | solution.py:114
  428.9 9.9 %multiply_convert_fusion.3 = bf16[12,512,64]{1,2,0:T(8,128)(2,1)} fusion(bf16[12,512,1024]{2,1,0:T(8,128)(2,1)} %get-tuple-element.108, bf16[3,12,1024,64]{2,3,1,0:T(8,128)(2,1)} %bitcast.73), kind=kOutput, calls=%fused_computation.89 | convolution fusion | flops 806092800 | bytes 14942208 | tf_op jit(solution)/shard_map/hqk,hke->hqe/dot_general | solution.py:114
  438.8 14.1 %fusion.46 = bf16[1,12,1024,64]{2,3,1,0:T(8,128)(2,1)} fusion(f32[12,1024,64]{1,2,0:T(8,128)} %fusion.13, f32[12,512]{1,0:T(8,128)S(1)} %copy-done.28, f32[12,512,1024]{2,1,0:T(8,128)} %get-tuple-element.93, pred[512,1024]{1,0:T(8,128)(4,1)S(1)} %copy-done.12, bf16[12,1024,64]{1,2,0:T(8,128)(2,1)} %bitcast.81), kind=kOutput, calls=%fused_computation.92 | convolution fusion | flops 832045056 | bytes 31219712 | tf_op jit(solution)/shard_map/hqk,hqe->hke/dot_general | solution.py:104
  453.2 7.1 fusion.62
  460.5 7.1 fusion.49
  476.4 9.9 %convolution_convert_fusion.2 = bf16[768,3072]{1,0:T(8,128)(2,1)} fusion(bf16[1024,3072]{1,0:T(8,128)(2,1)} %copy-done.50, f32[1024,768]{0,1:T(8,128)} %copy-done.4, f32[768]{0:T(1024)S(1)} %copy-done.44, f32[768]{0:T(1024)S(1)} %copy-done.35, f32[1024]{0:T(1024)S(1)} %add_rsqrt_fusion, f32[1024]{0:T(1024)S(1)} %broadcast_multiply_fusion.4), kind=kOutput, calls=%fused_computation.52 | convolution fusion | flops 4838129664 | bytes 14170112 | tf_op jit(solution)/shard_map/dot_general | solution.py:34
  487.8 9.8 %convolution_convert_fusion.1 = bf16[3072,768]{1,0:T(8,128)(2,1)} fusion(bf16[1024,3072]{1,0:T(8,128)(2,1)} %get-tuple-element.96, bf16[1024,768]{1,0:T(8,128)(2,1)S(1)} %copy-done.19), kind=kOutput, calls=%fused_computation.51 | convolution fusion | flops 4834197504 | bytes 12582912 | tf_op jit(solution)/shard_map/dot_general | solution.py:34
  499.5 9.1 %fusion.81 = (bf16[768]{0:T(1024)(128)(2,1)S(1)}, f32[1024,768]{1,0:T(8,128)}) fusion(bf16[1024,2304]{0,1:T(8,128)(2,1)} %bitcast.75, bf16[768,2304]{1,0:T(8,128)(2,1)} %all-gather.6.cloned.1.call-done), kind=kOutput, calls=%fused_computation.143 | convolution fusion | flops 3624664320 | bytes 11404800 | tf_op jit(solution)/shard_map/dot_general | solution.py:40
  523.5 18.8 %all-reduce.14 = (bf16[768]{0:T(1024)(128)(2,1)S(1)}, bf16[768]{0:T(1024)(128)(2,1)S(1)}, bf16[768]{0:T(1024)(128)(2,1)S(1)}, bf16[768]{0:T(1024)(128)(2,1)S(1)}...) all-reduce(bf16[768]{0:T(1024)(128)(2,1)S(1)} %dynamic-update-slice, ...), channel_id=1, replica_groups=mesh['dp'=8,'fsdp'=4] {'fsdp'}, use_global_device_ids=true, to_apply=%add.5 | all-reduce | flops 8448 | bytes 33792
  542.3 9.6 %add_convert_fusion.1 = bf16[1024,768]{0,1:T(8,128)(2,1)} fusion(f32[1024,768]{0,1:T(8,128)S(1)} %copy-done.6, bf16[1024,3072]{1,0:T(8,128)(2,1)} %get-tuple-element.96, bf16[3072,768]{1,0:T(8,128)(2,1)} %all-gather.12.cloned.1.call-done, f32[768]{0:T(1024)S(1)} %convert_element_type.161), kind=kOutput, calls=%fused_computation.77 | convolution fusion | flops 4834197504 | bytes 15731712 | tf_op jit(solution)/shard_map/dot_general | solution.py:183
  555.0 81.9 %reduce-scatter.9.cloned.1.call-done = bf16[192,3072]{1,0:T(8,128)(2,1)} async-done(((bf16[768,3072]{1,0:T(8,128)(2,1)}), bf16[192,3072]{1,0:T(8,128)(2,1)}) %reduce-scatter.9.cloned.1.call-update) | async-done | bytes 1179664 | tf_op jit(solution)/shard_map/reduce_scatter | solution.py:244
  636.9 88.1 %reduce-scatter.11.cloned.1.call-done = bf16[768,768]{1,0:T(8,128)(2,1)} async-done(((bf16[3072,768]{1,0:T(8,128)(2,1)}), bf16[768,768]{1,0:T(8,128)(2,1)}) %reduce-scatter.11.cloned.1.call-update) | async-done | bytes 1179664 | tf_op jit(solution)/shard_map/reduce_scatter | solution.py:250
  725.0 144.6 %all-reduce.17 = (f32[192]{0:T(256)}, f32[192]{0:T(256)}, f32[192,2304]{1,0:T(8,128)}, f32[192,768]{1,0:T(8,128)}, f32[192]{0:T(256)}, /*index=5*/f32[192]{0:T(2...) all-reduce(f32[192]{0:T(256)S(1)} %dynamic-slice_convert_fusion.6, ...), channel_id=1, replica_groups=mesh['dp'=8,'fsdp'=4] {'dp'}, use_global_device_ids=true, to_apply=%region_16.17 | all-reduce | flops 1771392 | bytes 10632192 | tf_op jit(solution)/shard_map/psum | solution.py:258
  (184 shorter events, 78.9 us)
Async XLA Ops:
  7.2 75.6 %all-gather.6.cloned.1.call-start = ((), (), s32[]{:S(2)}) async-start(), calls=%async_computation.4 | async-start | bytes 4423680 | tf_op jit(solution)/shard_map/all_gather | solution.py:148
  7.9 32.7 %copy-start.36 = (s32[1024]{0:T(1024)S(1)}, s32[1024]{0:T(1024)}, u32[]{:S(2)}) copy-start(s32[1024]{0:T(1024)} %param.15) | copy-start | bytes 12292
  7.9 33.9 %copy-start.46 = (bf16[768]{0:T(1024)(128)(2,1)S(1)}, bf16[768]{0:T(1024)(128)(2,1)}, u32[]{:S(2)}) copy-start(bf16[768]{0:T(1024)(128)(2,1)} %param.24) | copy-start | bytes 4612
  7.9 48.5 %copy-start.17 = (bf16[1024,768]{1,0:T(8,128)(2,1)S(1)}, bf16[1024,768]{1,0:T(8,128)(2,1)}, u32[]{:S(2)}) copy-start(bf16[1024,768]{1,0:T(8,128)(2,1)} %param.27) | copy-start | bytes 4718596
  7.9 168.4 %all-gather.8.cloned.1.call-start = ((), (), s32[]{:S(2)}) async-start(), calls=%async_computation.5 | async-start | bytes 1474560 | tf_op jit(solution)/shard_map/all_gather | solution.py:149
  8.7 194.7 %all-gather.10.cloned.1.call-start = ((), (), s32[]{:S(2)}) async-start(), calls=%async_computation.6 | async-start | bytes 5898240 | tf_op jit(solution)/shard_map/all_gather | solution.py:153
  9.4 283.2 %all-gather.12.cloned.1.call-start = ((), (), s32[]{:S(2)}) async-start(), calls=%async_computation.7 | async-start | bytes 5898240 | tf_op jit(solution)/shard_map/all_gather | solution.py:155
  10.0 545.0 %reduce-scatter.7.cloned.1.call-start = ((), (), s32[]{:S(2)}) async-start(), calls=%async_computation.9 | async-start | bytes 1474560 | tf_op jit(solution)/shard_map/reduce_scatter | solution.py:232
  38.1 44.7 %copy-start.31 = (f32[768]{0:T(1024)}, f32[768]{0:T(1024)S(1)}, u32[]{:S(2)}) copy-start(f32[768]{0:T(1024)S(1)} %convert_element_type.147) | copy-start | bytes 9220
  38.1 44.7 %copy-start.41 = (f32[768]{0:T(1024)}, f32[768]{0:T(1024)S(1)}, u32[]{:S(2)}) copy-start(f32[768]{0:T(1024)S(1)} %convert_element_type.148) | copy-start | bytes 9220
  39.8 136.6 %copy-start.2 = (bf16[1024,768]{0,1:T(8,128)(2,1)}, bf16[1024,768]{0,1:T(8,128)(2,1)S(1)}, u32[]{:S(2)}) copy-start(bf16[1024,768]{0,1:T(8,128)(2,1)S(1)} %copy.47) | copy-start | bytes 4718596
  40.1 50.5 %copy-start.29 = (f32[1024]{0:T(1024)}, f32[1024]{0:T(1024)S(1)}, u32[]{:S(2)}) copy-start(f32[1024]{0:T(1024)S(1)} %broadcast_multiply_fusion.5) | copy-start | bytes 12292
  40.6 50.0 %copy-start.33 = (f32[1024]{0:T(1024)}, f32[1024]{0:T(1024)S(1)}, u32[]{:S(2)}) copy-start(f32[1024]{0:T(1024)S(1)} %add_rsqrt_fusion.1) | copy-start | bytes 12292
  58.7 65.8 %copy-start.11 = (pred[512,1024]{1,0:T(8,128)(4,1)}, pred[512,1024]{1,0:T(8,128)(4,1)S(1)}, u32[]{:S(2)}) copy-start(pred[512,1024]{1,0:T(8,128)(4,1)S(1)} %get-tuple-element.84) | copy-start | bytes 1572868
  58.7 105.0 %copy-start.13 = (pred[512,1024]{1,0:T(8,128)(4,1)}, pred[512,1024]{1,0:T(8,128)(4,1)S(1)}, u32[]{:S(2)}) copy-start(pred[512,1024]{1,0:T(8,128)(4,1)S(1)} %get-tuple-element.85) | copy-start | bytes 1572868
  98.9 39.7 %copy-start.9 = (bf16[12,1024,64]{1,2,0:T(8,128)(2,1)}, bf16[12,1024,64]{1,2,0:T(8,128)(2,1)S(1)}, u32[]{:S(2)}) copy-start(bf16[12,1024,64]{1,2,0:T(8,128)(2,1)S(1)} %slice_bitcast_fusion.2) | copy-start | bytes 4718596
  111.5 16.6 %copy-start = (f32[12,512,1024]{2,1,0:T(8,128)S(1)}, f32[12,512,1024]{2,1,0:T(8,128)}, u32[]{:S(2)}) copy-start(f32[12,512,1024]{2,1,0:T(8,128)} %get-tuple-element.93) | copy-start | bytes 75497472
  151.3 15.6 %copy-start.1 = (f32[12,512,1024]{2,1,0:T(8,128)S(1)}, f32[12,512,1024]{2,1,0:T(8,128)}, u32[]{:S(2)}) copy-start(f32[12,512,1024]{2,1,0:T(8,128)} %get-tuple-element.91) | copy-start | bytes 75497472
  166.8 9.3 %copy-start.27 = (bf16[12,512,64]{1,2,0:T(8,128)(2,1)S(1)}, bf16[12,512,64]{1,2,0:T(8,128)(2,1)}, u32[]{:S(2)}) copy-start(bf16[12,512,64]{1,2,0:T(8,128)(2,1)} %fusion.51) | copy-start | bytes 2359300
  176.4 27.0 %copy-start.35 = (f32[768]{0:T(1024)S(1)}, f32[768]{0:T(1024)}, u32[]{:S(2)}) copy-start(f32[768]{0:T(1024)} %convert_element_type.156) | copy-start | bytes 9220
  176.4 27.0 %copy-start.37 = (f32[4,1,768]{2,1,0:T(1,128)S(1)}, f32[4,1,768]{2,1,0:T(1,128)}, u32[]{:S(2)}) copy-start(f32[4,1,768]{2,1,0:T(1,128)} %convert_element_type.192) | copy-start | bytes 36868
  176.4 27.0 %copy-start.43 = (f32[768]{0:T(1024)S(1)}, f32[768]{0:T(1024)}, u32[]{:S(2)}) copy-start(f32[768]{0:T(1024)} %convert_element_type.157) | copy-start | bytes 9220
  203.4 89.3 %copy-start.18 = (bf16[1024,768]{1,0:T(8,128)(2,1)S(1)}, bf16[1024,768]{1,0:T(8,128)(2,1)}, u32[]{:S(2)}) copy-start(bf16[1024,768]{1,0:T(8,128)(2,1)} %param.27) | copy-start | bytes 4718596
  292.7 12.5 %copy-start.47 = (bf16[768,3072]{1,0:T(8,128)(2,1)S(1)}, bf16[768,3072]{1,0:T(8,128)(2,1)}, u32[]{:S(2)}) copy-start(bf16[768,3072]{1,0:T(8,128)(2,1)} %all-gather.10.cloned.1.call-done) | copy-start | bytes 14155780
  323.4 20.8 %copy-start.25 = (bf16[1024,768]{0,1:T(8,128)(2,1)}, bf16[1024,768]{0,1:T(8,128)(2,1)S(1)}, u32[]{:S(2)}) copy-start(bf16[1024,768]{0,1:T(8,128)(2,1)S(1)} %convolution_convert_fusion.4) | copy-start | bytes 4718596
  344.2 13.4 %copy-start.16 = (f32[1024,768]{0,1:T(8,128)S(1)}, f32[1024,768]{0,1:T(8,128)}, u32[]{:S(2)}) copy-start(f32[1024,768]{0,1:T(8,128)} %copy-done.15) | copy-start | bytes 9437188
  344.2 13.4 %copy-start.24 = (bf16[12,1024,64]{1,2,0:T(8,128)(2,1)S(1)}, bf16[12,1024,64]{1,2,0:T(8,128)(2,1)}, u32[]{:S(2)}) copy-start(bf16[12,1024,64]{1,2,0:T(8,128)(2,1)} %copy-done.23) | copy-start | bytes 4718596
  438.8 14.4 %copy-start.10 = (bf16[12,1024,64]{1,2,0:T(8,128)(2,1)S(1)}, bf16[12,1024,64]{1,2,0:T(8,128)(2,1)}, u32[]{:S(2)}) copy-start(bf16[12,1024,64]{1,2,0:T(8,128)(2,1)} %copy-done.9) | copy-start | bytes 4718596
  452.9 102.1 %reduce-scatter.5.cloned.1.call-start = ((), (), s32[]{:S(2)}) async-start(), calls=%async_computation.8 | async-start | bytes 4423680 | tf_op jit(solution)/shard_map/reduce_scatter | solution.py:229
  476.3 160.5 %reduce-scatter.9.cloned.1.call-start = ((), (), s32[]{:S(2)}) async-start(), calls=%async_computation.10 | async-start | bytes 5898240 | tf_op jit(solution)/shard_map/reduce_scatter | solution.py:244
  486.3 238.7 %reduce-scatter.11.cloned.1.call-start = ((), (), s32[]{:S(2)}) async-start(), calls=%async_computation.11 | async-start | bytes 5898240 | tf_op jit(solution)/shard_map/reduce_scatter | solution.py:250
  519.8 22.5 %copy-start.6 = (f32[1024,768]{0,1:T(8,128)S(1)}, f32[1024,768]{0,1:T(8,128)}, u32[]{:S(2)}) copy-start(f32[1024,768]{0,1:T(8,128)} %copy-done.4) | copy-start | bytes 9437188
  (27 other events, 91.2 us)
Sparse Core Ops, SparseCore 0:
  9.6 73.1 all-gather.5
  84.4 28.7 all-gather.7
  114.7 88.6 all-gather.9
  204.8 87.7 all-gather.11
  453.0 27.7 reduce-scatter.6
  483.0 66.1 reduce-scatter.4
  551.4 85.4 reduce-scatter.8
  639.2 85.7 reduce-scatter.10
where the time goes:
time: 880 us; the launch traced here: 877 us
  waiting for transfers between devices  269 us (31%)
  matrix products  262 us (30%)
  blocking collectives  199 us (23%)
  other arithmetic  86.3 us (10%)
  local copies, waits for them, and re-layouts  43 us (5%)
  between operations  16.9 us (2%)
    psum x1, blocking collectives, on_device(): lax.psum((all_rows[0], all_rows[1], all_rows[2], all_rows[3], all_rows[4]...  145 us
    reduce_scatter x1, waiting for transfers between devices, on_device(): lax.psum_scatter(d_w_fc2.astype(jnp.bfloat16), 'fsdp', scatter_dimension=...  88.1 us
    reduce_scatter x1, waiting for transfers between devices, on_device(): lax.psum_scatter(d_w_fc1.astype(jnp.bfloat16), 'fsdp', scatter_dimension=...  81.9 us
    all_gather x1, waiting for transfers between devices, on_device(): lax.all_gather(w_fc2, 'fsdp', axis=0, tiled=True)  50.3 us
    convert_element_type x1, other arithmetic, attend_back(): d_score = (attn_probs * (d_probs - jnp.sum(d_probs * attn_probs, axis=-1,...  41.8 us
    unnamed x2, blocking collectives  40.6 us
    dot_general x1, matrix products, on_device(): jnp.dot(normed_mid, gathered[7], preferred_element_type=jnp.float32)  39 us
    dot_general x2, matrix products, attend_back(): jnp.einsum('hqe,hke->hqk', grad_block, value_heads, preferred_element_typ...  38.8 us
  transfers between devices with their start and end apart: 8, of which 5 were waited for; matrix products, arithmetic and copies ran while one was open for 25% of the time, Pallas kernels for 0%

commit v1 on v0

--- a/solution.py
+++ b/solution.py
@@ -9,6 +9,18 @@
 neg_big = -1e30
 inv_sqrt_two = 1.0 / math.sqrt(2.0)
 inv_sqrt_tau = 1.0 / math.sqrt(2.0 * math.pi)
+
+
+def ring_gather(shard, axis, dim):
+    ways, here, step = (lax.axis_size(axis), lax.axis_index(axis), shard.shape[dim])
+    shape = [n * ways if d == dim else n for d, n in enumerate(shard.shape)]
+    full = lax.dynamic_update_slice_in_dim(
+        jnp.zeros(shape, shard.dtype), shard, here * step, axis=dim
+    )
+    for far in range(1, ways):
+        shard = lax.ppermute(shard, axis, [(d, (d + 1) % ways) for d in range(ways)])
+        full = lax.dynamic_update_slice_in_dim(full, shard, (here - far) % ways * step, axis=dim)
+    return full
 
 
 def layer_norm(token_rows, gain_vec, shift_vec):
@@ -152,7 +164,7 @@
         lax.all_gather(ln2_bias, "fsdp", axis=0, tiled=True),
         lax.all_gather(w_fc1, "fsdp", axis=0, tiled=True),
         lax.all_gather(b_fc1, "fsdp", axis=0, tiled=True),
-        lax.all_gather(w_fc2, "fsdp", axis=0, tiled=True),
+        ring_gather(w_fc2, "fsdp", 0),
         lax.all_gather(b_fc2, "fsdp", axis=0, tiled=True),
     )
     gain_one = gathered[0].astype(jnp.float32)

time: 880 us -> 944 us (1.073)
  starting transfers between devices: 1.03 us -> 29.5 us
  blocking collectives: 199 us -> 220 us
  local copies, waits for them, and re-layouts: 43 us -> 54.2 us
    ppermute x0 -> x3, waiting for transfers between devices: none -> 143 us  [ring_gather(): lax.ppermute(shard, axis, [(d, (d + 1) % ways) for d in range(ways)])]
    reduce_scatter x1, waiting for transfers between devices: 81.9 us -> 0.01 us  [on_device(): lax.psum_scatter(d_w_fc1.astype(jnp.bfloat16), 'fsdp', scatter_dimension=...]
    reduce_scatter x1, waiting for transfers between devices: 88.1 us -> 31.5 us  [on_device(): lax.psum_scatter(d_w_fc2.astype(jnp.bfloat16), 'fsdp', scatter_dimension=...]
    ppermute x0 -> x3, starting transfers between devices: none -> 28.8 us  [ring_gather(): lax.ppermute(shard, axis, [(d, (d + 1) % ways) for d in range(ways)])]
    unnamed x2, blocking collectives: 40.6 us -> 61.8 us
    unnamed x120 -> x128, local copies, waits for them, and re-layouts: 27.5 us -> 29.2 us
  transfers between devices with their start and end apart: 8 -> 11, of which waited for: 5 -> 7; matrix products, arithmetic and copies ran while one was open for 25% -> 24% of each run, Pallas kernels for 0% -> 0%
where the time goes in v1:
time: 944 us; the launch traced here: 941 us
  waiting for transfers between devices  272 us (29%)
  matrix products  261 us (28%)
  blocking collectives  220 us (23%)
  other arithmetic  86.4 us (9%)
  local copies, waits for them, and re-layouts  54.2 us (6%)
  starting transfers between devices  29.5 us (3%)
  between operations  17 us (2%)
    psum x1, blocking collectives, on_device(): lax.psum((all_rows[0], all_rows[1], all_rows[2], all_rows[3], all_rows[4]...  145 us
    ppermute x3, waiting for transfers between devices, ring_gather(): lax.ppermute(shard, axis, [(d, (d + 1) % ways) for d in range(ways)])  143 us
    unnamed x2, blocking collectives  61.8 us
    all_gather x1, waiting for transfers between devices, on_device(): lax.all_gather(w_fc2, 'fsdp', axis=0, tiled=True)  50.3 us
    convert_element_type x1, other arithmetic, attend_back(): d_score = (attn_probs * (d_probs - jnp.sum(d_probs * attn_probs, axis=-1,...  41.8 us
    dot_general x1, matrix products, on_device(): jnp.dot(normed_mid, gathered[7], preferred_element_type=jnp.float32)  39 us
    dot_general x2, matrix products, attend_back(): jnp.einsum('hqe,hke->hqk', grad_block, value_heads, preferred_element_typ...  38.9 us
    reduce_scatter x1, waiting for transfers between devices, on_device(): lax.psum_scatter(d_w_fc2.astype(jnp.bfloat16), 'fsdp', scatter_dimension=...  31.5 us
  transfers between devices with their start and end apart: 11, of which 7 were waited for; matrix products, arithmetic and copies ran while one was open for 24% of the time, Pallas kernels for 0%

profile of v1, /device:TPU:0, one launch (start us, length us, event | category | flops | bytes accessed | tf_op | source)
XLA Modules:
  0.0 940.6 jit_solution(10659164305915748822)
XLA Ops:
  16.2 21.8 %all-reduce.15 = (bf16[768]{0:T(1024)(128)(2,1)S(1)}, bf16[768]{0:T(1024)(128)(2,1)S(1)}, bf16[768]{0:T(1024)(128)(2,1)S(1)}, bf16[768]{0:T(1024)(128)(2,1)S(1)}, bf16[768]{0:T(1024)(128)(2,1)S(1)}) all-reduce(bf16[768]{0:T(1024)(128)(2,1)S(1)} %dynamic-update-slice.1, ...), channel_id=1, replica_groups=mesh['dp'=8,'fsdp'=4] {'fsdp'}, use_global_device_ids=true, to_apply=%add.1 | all-reduce | flops 3840 | bytes 15360
  41.8 14.0 %all-gather = bf16[4,1,768]{2,1,0:T(2,128)(2,1)S(1)} all-gather(bf16[1,1,768]{2,1,0:T(2,128)(2,1)S(1)} %reshape.178), channel_id=1, replica_groups=mesh['dp'=8,'fsdp'=4] {'fsdp'}, dimensions={0}, use_global_device_ids=true | all-gather | bytes 7680 | tf_op jit(solution)/shard_map/all_gather | solution.py:166
  58.7 24.1 %all-gather.6.cloned.1.call-done = bf16[768,2304]{1,0:T(8,128)(2,1)} async-done(((bf16[192,2304]{1,0:T(8,128)(2,1)}), bf16[768,2304]{1,0:T(8,128)(2,1)}) %all-gather.6.cloned.1.call-update) | async-done | bytes 3538960 | tf_op jit(solution)/shard_map/all_gather | solution.py:160
  98.9 12.6 %fusion.28 = (f32[12,512]{1,0:T(8,128)S(1)}, f32[12,512,1024]{2,1,0:T(8,128)}) fusion(pred[512,1024]{1,0:T(8,128)(4,1)S(1)} %get-tuple-element.84, bf16[3,12,1024,64]{2,3,1,0:T(8,128)(2,1)} %bitcast.66, bf16[12,1024,64]{1,2,0:T(8,128)(2,1)S(1)} %slice_bitcast_fusion.2), kind=kOutput, calls=%fused_computation.48 | convolution fusion | flops 824174592 | bytes 28073984 | tf_op jit(solution)/shard_map/hqe,hke->hqk/dot_general | solution.py:66
  111.6 12.9 %fusion = f32[12,512]{1,0:T(8,128)S(1)} fusion(f32[12,512]{1,0:T(8,128)S(1)} %get-tuple-element.92, f32[12,512,1024]{2,1,0:T(8,128)} %get-tuple-element.93, pred[512,1024]{1,0:T(8,128)(4,1)S(1)} %get-tuple-element.84), kind=kLoop, calls=%fused_computation.12 | loop fusion | flops 25159680 | bytes 25739264 | tf_op jit(solution)/shard_map/reduce_sum | solution.py:89
  128.2 9.9 %fusion.51 = bf16[12,512,64]{1,2,0:T(8,128)(2,1)} fusion(f32[12,512]{1,0:T(8,128)S(1)} %fusion, f32[12,512]{1,0:T(8,128)S(1)} %get-tuple-element.92, f32[12,512,1024]{2,1,0:T(8,128)S(1)} %copy-done, pred[512,1024]{1,0:T(8,128)(4,1)S(1)} %get-tuple-element.84, bf16[3,12,1024,64]{2,3,1,0:T(8,128)(2,1)} %bitcast.67), kind=kOutput, calls=%fused_computation.95 | convolution fusion | flops 837156864 | bytes 28098560 | tf_op jit(solution)/shard_map/hqk,hke->hqe/dot_general | solution.py:92
  138.7 12.6 %fusion.29 = (f32[12,512]{1,0:T(8,128)S(1)}, f32[12,512,1024]{2,1,0:T(8,128)}) fusion(pred[512,1024]{1,0:T(8,128)(4,1)S(1)} %get-tuple-element.85, bf16[3,12,1024,64]{2,3,1,0:T(8,128)(2,1)} %bitcast.68, bf16[12,1024,64]{1,2,0:T(8,128)(2,1)S(1)} %slice_bitcast_fusion.2), kind=kOutput, calls=%fused_computation.49 | convolution fusion | flops 824174592 | bytes 28073984 | tf_op jit(solution)/shard_map/hqe,hke->hqk/dot_general | solution.py:66
  151.4 12.4 %fusion.1 = f32[12,512]{1,0:T(8,128)S(1)} fusion(f32[12,512]{1,0:T(8,128)S(1)} %get-tuple-element.90, f32[12,512,1024]{2,1,0:T(8,128)} %get-tuple-element.91, pred[512,1024]{1,0:T(8,128)(4,1)S(1)} %get-tuple-element.85), kind=kLoop, calls=%fused_computation.13 | loop fusion | flops 25159680 | bytes 25739264 | tf_op jit(solution)/shard_map/reduce_sum | solution.py:89
  166.9 9.3 fusion.50
  182.0 21.4 %all-gather.10.cloned.1.call-done = bf16[768,3072]{1,0:T(8,128)(2,1)} async-done(((bf16[192,3072]{1,0:T(8,128)(2,1)}), bf16[768,3072]{1,0:T(8,128)(2,1)}) %all-gather.10.cloned.1.call-update) | async-done | bytes 4718608 | tf_op jit(solution)/shard_map/all_gather | solution.py:165
  203.4 39.0 %fusion.6 = (bf16[1024,3072]{1,0:T(8,128)(2,1)}, f32[1024,3072]{1,0:T(8,128)}) fusion(f32[3072]{0:T(1024)S(1)} %bitcast.82, bf16[768,3072]{1,0:T(8,128)(2,1)} %all-gather.10.cloned.1.call-done, f32[1024,768]{0,1:T(8,128)} %copy-done.4, f32[768]{0:T(1024)S(1)} %copy-done.46, f32[768]{0:T(1024)S(1)} %copy-done.38, f32[1024]{0:T(1024)S(1)} %add_rsqrt_fusion, ...), kind=kOutput, calls=%fused_computation.20 | convolution fusion | flops 5043388416 | bytes 26765312 | tf_op jit(solution)/shard_map/dot_general | solution.py:190
  242.4 50.3 %all-gather.12.cloned.1.call-done = bf16[3072,768]{1,0:T(8,128)(2,1)} async-done(((bf16[768,768]{1,0:T(8,128)(2,1)}), bf16[3072,768]{1,0:T(8,128)(2,1)}) %all-gather.12.cloned.1.call-update) | async-done | bytes 4718608 | tf_op jit(solution)/shard_map/all_gather | solution.py:208
  292.7 12.5 %fusion.83 = (bf16[3072]{0:T(1024)(128)(2,1)}, bf16[1024,3072]{1,0:T(8,128)(2,1)S(1)}) fusion(f32[1024,3072]{1,0:T(8,128)} %get-tuple-element.97, f32[3072]{0:T(1024)S(1)} %bitcast.83, bf16[1024,768]{1,0:T(8,128)(2,1)S(1)} %copy-done.18, bf16[3072,768]{1,0:T(8,128)(2,1)} %all-gather.12.cloned.1.call-done), kind=kOutput, calls=%fused_computation.149 | convolution fusion | flops 4869583872 | bytes 25184256 | tf_op jit(solution)/shard_map/dot_general | solution.py:52
  323.4 20.8 %multiply_reduce_fusion = (f32[12,512]{1,0:T(8,128)S(1)}, f32[12,512,1024]{2,1,0:T(8,128)}) fusion(f32[12,512]{1,0:T(8,128)S(1)} %log_add_fusion, f32[12,512,1024]{2,1,0:T(8,128)} %get-tuple-element.91, pred[512,1024]{1,0:T(8,128)(4,1)S(1)} %copy-done.14, bf16[3,12,1024,64]{2,3,1,0:T(8,128)(2,1)} %bitcast.70, bf16[12,1024,64]{1,2,0:T(8,128)(2,1)S(1)} %bitcast.78), kind=kOutput, calls=%fused_computation.1 | convolution fusion | flops 836757504 | bytes 53272576 | tf_op jit(solution)/shard_map/hqe,hke->hqk/dot_general | solution.py:119
  344.2 13.4 %fusion.13 = f32[12,1024,64]{1,2,0:T(8,128)} fusion(f32[12,512]{1,0:T(8,128)S(1)} %log_add_fusion, f32[12,512,1024]{2,1,0:T(8,128)} %get-tuple-element.91, pred[512,1024]{1,0:T(8,128)(4,1)S(1)} %copy-done.14, bf16[12,1024,64]{1,2,0:T(8,128)(2,1)S(1)} %bitcast.79), kind=kOutput, calls=%fused_computation.27 | convolution fusion | flops 830472192 | bytes 29655040 | tf_op jit(solution)/shard_map/hqk,hqe->hke/dot_general | solution.py:116
  360.1 18.1 %multiply_reduce_fusion.1 = (f32[12,512]{1,0:T(8,128)S(1)}, f32[12,512,1024]{2,1,0:T(8,128)}) fusion(f32[12,512]{1,0:T(8,128)S(1)} %copy-done.31, f32[12,512,1024]{2,1,0:T(8,128)} %get-tuple-element.93, pred[512,1024]{1,0:T(8,128)(4,1)S(1)} %copy-done.12, bf16[3,12,1024,64]{2,3,1,0:T(8,128)(2,1)} %bitcast.71, bf16[12,1024,64]{1,2,0:T(8,128)(2,1)} %bitcast.80), kind=kOutput, calls=%fused_computation.4 | convolution fusion | flops 836757504 | bytes 53264384 | tf_op jit(solution)/shard_map/hqe,hke->hqk/dot_general | solution.py:119
  378.2 41.8 %multiply_convert_fusion = (bf16[12,512,1024]{2,1,0:T(8,128)(2,1)}, bf16[12,512,1024]{2,1,0:T(8,128)(2,1)}) fusion(f32[12,512,1024]{2,1,0:T(8,128)} %get-tuple-element.101, f32[12,512]{1,0:T(8,128)S(1)} %get-tuple-element.100, f32[12,512]{1,0:T(8,128)S(1)} %log_add_fusion, f32[12,512,1024]{2,1,0:T(8,128)} %get-tuple-element.91, ...), kind=kLoop, calls=%fused_computation | loop fusion | flops 75497472 | bytes 126976000 | tf_op jit(solution)/shard_map/convert_element_type | solution.py:124
  420.1 8.9 multiply_convert_fusion.4
  429.0 9.9 %multiply_convert_fusion.3 = bf16[12,512,64]{1,2,0:T(8,128)(2,1)} fusion(bf16[12,512,1024]{2,1,0:T(8,128)(2,1)} %get-tuple-element.108, bf16[3,12,1024,64]{2,3,1,0:T(8,128)(2,1)} %bitcast.73), kind=kOutput, calls=%fused_computation.89 | convolution fusion | flops 806092800 | bytes 14942208 | tf_op jit(solution)/shard_map/hqk,hke->hqe/dot_general | solution.py:126
  438.9 14.1 %fusion.46 = bf16[1,12,1024,64]{2,3,1,0:T(8,128)(2,1)} fusion(f32[12,1024,64]{1,2,0:T(8,128)} %fusion.13, f32[12,512]{1,0:T(8,128)S(1)} %copy-done.31, f32[12,512,1024]{2,1,0:T(8,128)} %get-tuple-element.93, pred[512,1024]{1,0:T(8,128)(4,1)S(1)} %copy-done.12, bf16[12,1024,64]{1,2,0:T(8,128)(2,1)} %bitcast.81), kind=kOutput, calls=%fused_computation.92 | convolution fusion | flops 832045056 | bytes 31219712 | tf_op jit(solution)/shard_map/hqk,hqe->hke/dot_general | solution.py:116
  476.7 9.8 %convolution_convert_fusion.2 = bf16[768,3072]{1,0:T(8,128)(2,1)} fusion(bf16[1024,3072]{1,0:T(8,128)(2,1)} %copy-done.54, f32[1024,768]{0,1:T(8,128)} %copy-done.4, f32[768]{0:T(1024)S(1)} %copy-done.47, f32[768]{0:T(1024)S(1)} %copy-done.38, f32[1024]{0:T(1024)S(1)} %add_rsqrt_fusion, f32[1024]{0:T(1024)S(1)} %broadcast_multiply_fusion.4), kind=kOutput, calls=%fused_computation.52 | convolution fusion | flops 4838129664 | bytes 14170112 | tf_op jit(solution)/shard_map/dot_general | solution.py:46
  488.3 9.8 %convolution_convert_fusion.1 = bf16[3072,768]{1,0:T(8,128)(2,1)} fusion(bf16[1024,3072]{1,0:T(8,128)(2,1)} %get-tuple-element.96, bf16[1024,768]{1,0:T(8,128)(2,1)S(1)} %copy-done.19), kind=kOutput, calls=%fused_computation.51 | convolution fusion | flops 4834197504 | bytes 12582912 | tf_op jit(solution)/shard_map/dot_general | solution.py:46
  498.1 55.7 %collective-permute-done = bf16[768,768]{1,0:T(8,128)(2,1)S(1)} collective-permute-done((bf16[768,768]{1,0:T(8,128)(2,1)}, bf16[768,768]{1,0:T(8,128)(2,1)S(1)}, u32[]{:S(2)}, u32[]{:S(2)}) %collective-permute-start) | collective-permute-done | bytes 1179680 | tf_op jit(solution)/shard_map/ppermute | solution.py:21
  554.9 15.3 %collective-permute-start.1 = (bf16[768,768]{1,0:T(8,128)(2,1)S(1)}, bf16[768,768]{1,0:T(8,128)(2,1)}, u32[]{:S(2)}, u32[]{:S(2)}) collective-permute-start(bf16[768,768]{1,0:T(8,128)(2,1)S(1)} %collective-permute-done), channel_id=1, source_target_pairs={{0,1},{1,2},{2,3},{3,0},{4,5},{5,6},{6,7},{7,4},{8,9},{9,10},{10,1... | collective-permute-start | bytes 3538952 | tf_op jit(solution)/shard_map/ppermute | solution.py:21
  570.1 43.2 %collective-permute-done.1 = bf16[768,768]{1,0:T(8,128)(2,1)} collective-permute-done((bf16[768,768]{1,0:T(8,128)(2,1)S(1)}, bf16[768,768]{1,0:T(8,128)(2,1)}, u32[]{:S(2)}, u32[]{:S(2)}) %collective-permute-start.1) | collective-permute-done | bytes 1179680 | tf_op jit(solution)/shard_map/ppermute | solution.py:21
  613.3 13.5 %collective-permute-start.2 = (bf16[768,768]{1,0:T(8,128)(2,1)}, bf16[768,768]{1,0:T(8,128)(2,1)}, u32[]{:S(2)}, u32[]{:S(2)}) collective-permute-start(bf16[768,768]{1,0:T(8,128)(2,1)} %collective-permute-done.1), channel_id=1, source_target_pairs={{0,1},{1,2},{2,3},{3,0},{4,5},{5,6},{6,7},{7,4},{8,9},{9,10},{10,1... | collective-permute-start | bytes 3538952 | tf_op jit(solution)/shard_map/ppermute | solution.py:21
  635.7 43.8 %collective-permute-done.2 = bf16[768,768]{1,0:T(8,128)(2,1)} collective-permute-done((bf16[768,768]{1,0:T(8,128)(2,1)}, bf16[768,768]{1,0:T(8,128)(2,1)}, u32[]{:S(2)}, u32[]{:S(2)}) %collective-permute-start.2) | collective-permute-done | bytes 1179680 | tf_op jit(solution)/shard_map/ppermute | solution.py:21
  681.8 8.0 fusion.81
  704.8 39.9 %all-reduce.14 = (bf16[768]{0:T(1024)(128)(2,1)S(1)}, bf16[768]{0:T(1024)(128)(2,1)S(1)}, bf16[768]{0:T(1024)(128)(2,1)S(1)}, bf16[768]{0:T(1024)(128)(2,1)S(1)}...) all-reduce(bf16[768]{0:T(1024)(128)(2,1)S(1)} %dynamic-update-slice, ...), channel_id=1, replica_groups=mesh['dp'=8,'fsdp'=4] {'fsdp'}, use_global_device_ids=true, to_apply=%add.5 | all-reduce | flops 8448 | bytes 33792
  744.8 9.5 %add_convert_fusion.1 = bf16[1024,768]{0,1:T(8,128)(2,1)} fusion(f32[1024,768]{0,1:T(8,128)S(1)} %copy-done.6, bf16[1024,3072]{1,0:T(8,128)(2,1)} %get-tuple-element.96, bf16[3072,768]{1,0:T(8,128)(2,1)} %constant_dynamic-update-slice_fusion, f32[768]{0:T(1024)S(1)} %convert_element_type.161), kind=kOutput, calls=%fused_computation.77 | convolution fusion | flops 4834197504 | bytes 15731712 | tf_op jit(solution)/shard_map/dot_general | solution.py:195
  757.4 31.5 %reduce-scatter.11.cloned.1.call-done = bf16[768,768]{1,0:T(8,128)(2,1)} async-done(((bf16[3072,768]{1,0:T(8,128)(2,1)}), bf16[768,768]{1,0:T(8,128)(2,1)}) %reduce-scatter.11.cloned.1.call-update) | async-done | bytes 1179664 | tf_op jit(solution)/shard_map/reduce_scatter | solution.py:262
  788.9 144.6 %all-reduce.17 = (f32[192]{0:T(256)}, f32[192]{0:T(256)}, f32[192,2304]{1,0:T(8,128)}, f32[192,768]{1,0:T(8,128)}, f32[192]{0:T(256)}, /*index=5*/f32[192]{0:T(2...) all-reduce(f32[192]{0:T(256)S(1)} %dynamic-slice_convert_fusion.6, ...), channel_id=1, replica_groups=mesh['dp'=8,'fsdp'=4] {'dp'}, use_global_device_ids=true, to_apply=%region_16.17 | all-reduce | flops 1771392 | bytes 10632192 | tf_op jit(solution)/shard_map/psum | solution.py:270
  (203 shorter events, 119.3 us)
Async XLA Ops:
  7.2 75.6 %all-gather.6.cloned.1.call-start = ((), (), s32[]{:S(2)}) async-start(), calls=%async_computation.4 | async-start | bytes 4423680 | tf_op jit(solution)/shard_map/all_gather | solution.py:160
  7.9 32.7 %copy-start.39 = (s32[1024]{0:T(1024)S(1)}, s32[1024]{0:T(1024)}, u32[]{:S(2)}) copy-start(s32[1024]{0:T(1024)} %param.15) | copy-start | bytes 12292
  7.9 33.9 %copy-start.49 = (bf16[768]{0:T(1024)(128)(2,1)S(1)}, bf16[768]{0:T(1024)(128)(2,1)}, u32[]{:S(2)}) copy-start(bf16[768]{0:T(1024)(128)(2,1)} %param.24) | copy-start | bytes 4612
  7.9 48.5 %copy-start.17 = (bf16[1024,768]{1,0:T(8,128)(2,1)S(1)}, bf16[1024,768]{1,0:T(8,128)(2,1)}, u32[]{:S(2)}) copy-start(bf16[1024,768]{1,0:T(8,128)(2,1)} %param.27) | copy-start | bytes 4718596
  7.9 168.5 %all-gather.8.cloned.1.call-start = ((), (), s32[]{:S(2)}) async-start(), calls=%async_computation.5 | async-start | bytes 1474560 | tf_op jit(solution)/shard_map/all_gather | solution.py:161
  8.7 194.7 %all-gather.10.cloned.1.call-start = ((), (), s32[]{:S(2)}) async-start(), calls=%async_computation.6 | async-start | bytes 5898240 | tf_op jit(solution)/shard_map/all_gather | solution.py:165
  9.4 283.2 %all-gather.12.cloned.1.call-start = ((), (), s32[]{:S(2)}) async-start(), calls=%async_computation.7 | async-start | bytes 5898240 | tf_op jit(solution)/shard_map/all_gather | solution.py:208
  10.0 747.4 %reduce-scatter.7.cloned.1.call-start = ((), (), s32[]{:S(2)}) async-start(), calls=%async_computation.9 | async-start | bytes 1474560 | tf_op jit(solution)/shard_map/reduce_scatter | solution.py:244
  38.1 44.7 %copy-start.34 = (f32[768]{0:T(1024)}, f32[768]{0:T(1024)S(1)}, u32[]{:S(2)}) copy-start(f32[768]{0:T(1024)S(1)} %convert_element_type.147) | copy-start | bytes 9220
  38.1 44.7 %copy-start.44 = (f32[768]{0:T(1024)}, f32[768]{0:T(1024)S(1)}, u32[]{:S(2)}) copy-start(f32[768]{0:T(1024)S(1)} %convert_element_type.148) | copy-start | bytes 9220
  39.8 136.7 %copy-start.2 = (bf16[1024,768]{0,1:T(8,128)(2,1)}, bf16[1024,768]{0,1:T(8,128)(2,1)S(1)}, u32[]{:S(2)}) copy-start(bf16[1024,768]{0,1:T(8,128)(2,1)S(1)} %copy.47) | copy-start | bytes 4718596
  40.1 50.5 %copy-start.32 = (f32[1024]{0:T(1024)}, f32[1024]{0:T(1024)S(1)}, u32[]{:S(2)}) copy-start(f32[1024]{0:T(1024)S(1)} %broadcast_multiply_fusion.5) | copy-start | bytes 12292
  40.6 50.0 %copy-start.36 = (f32[1024]{0:T(1024)}, f32[1024]{0:T(1024)S(1)}, u32[]{:S(2)}) copy-start(f32[1024]{0:T(1024)S(1)} %add_rsqrt_fusion.1) | copy-start | bytes 12292
  58.7 65.9 %copy-start.11 = (pred[512,1024]{1,0:T(8,128)(4,1)}, pred[512,1024]{1,0:T(8,128)(4,1)S(1)}, u32[]{:S(2)}) copy-start(pred[512,1024]{1,0:T(8,128)(4,1)S(1)} %get-tuple-element.84) | copy-start | bytes 1572868
  58.7 105.1 %copy-start.13 = (pred[512,1024]{1,0:T(8,128)(4,1)}, pred[512,1024]{1,0:T(8,128)(4,1)S(1)}, u32[]{:S(2)}) copy-start(pred[512,1024]{1,0:T(8,128)(4,1)S(1)} %get-tuple-element.85) | copy-start | bytes 1572868
  98.9 39.8 %copy-start.9 = (bf16[12,1024,64]{1,2,0:T(8,128)(2,1)}, bf16[12,1024,64]{1,2,0:T(8,128)(2,1)S(1)}, u32[]{:S(2)}) copy-start(bf16[12,1024,64]{1,2,0:T(8,128)(2,1)S(1)} %slice_bitcast_fusion.2) | copy-start | bytes 4718596
  111.6 16.6 %copy-start = (f32[12,512,1024]{2,1,0:T(8,128)S(1)}, f32[12,512,1024]{2,1,0:T(8,128)}, u32[]{:S(2)}) copy-start(f32[12,512,1024]{2,1,0:T(8,128)} %get-tuple-element.93) | copy-start | bytes 75497472
  151.4 15.6 %copy-start.1 = (f32[12,512,1024]{2,1,0:T(8,128)S(1)}, f32[12,512,1024]{2,1,0:T(8,128)}, u32[]{:S(2)}) copy-start(f32[12,512,1024]{2,1,0:T(8,128)} %get-tuple-element.91) | copy-start | bytes 75497472
  176.5 26.9 %copy-start.38 = (f32[768]{0:T(1024)S(1)}, f32[768]{0:T(1024)}, u32[]{:S(2)}) copy-start(f32[768]{0:T(1024)} %convert_element_type.156) | copy-start | bytes 9220
  176.5 26.9 %copy-start.40 = (f32[4,1,768]{2,1,0:T(1,128)S(1)}, f32[4,1,768]{2,1,0:T(1,128)}, u32[]{:S(2)}) copy-start(f32[4,1,768]{2,1,0:T(1,128)} %convert_element_type.192) | copy-start | bytes 36868
  176.5 26.9 %copy-start.46 = (f32[768]{0:T(1024)S(1)}, f32[768]{0:T(1024)}, u32[]{:S(2)}) copy-start(f32[768]{0:T(1024)} %convert_element_type.157) | copy-start | bytes 9220
  203.4 89.3 %copy-start.18 = (bf16[1024,768]{1,0:T(8,128)(2,1)S(1)}, bf16[1024,768]{1,0:T(8,128)(2,1)}, u32[]{:S(2)}) copy-start(bf16[1024,768]{1,0:T(8,128)(2,1)} %param.27) | copy-start | bytes 4718596
  323.4 20.8 %copy-start.26 = (bf16[1024,768]{0,1:T(8,128)(2,1)}, bf16[1024,768]{0,1:T(8,128)(2,1)S(1)}, u32[]{:S(2)}) copy-start(bf16[1024,768]{0,1:T(8,128)(2,1)S(1)} %convolution_convert_fusion.4) | copy-start | bytes 4718596
  453.0 304.4 %reduce-scatter.5.cloned.1.call-start = ((), (), s32[]{:S(2)}) async-start(), calls=%async_computation.8 | async-start | bytes 4423680 | tf_op jit(solution)/shard_map/reduce_scatter | solution.py:241
  476.6 280.8 %reduce-scatter.9.cloned.1.call-start = ((), (), s32[]{:S(2)}) async-start(), calls=%async_computation.10 | async-start | bytes 5898240 | tf_op jit(solution)/shard_map/reduce_scatter | solution.py:256
  486.5 302.3 %reduce-scatter.11.cloned.1.call-start = ((), (), s32[]{:S(2)}) async-start(), calls=%async_computation.11 | async-start | bytes 5898240 | tf_op jit(solution)/shard_map/reduce_scatter | solution.py:262
  498.0 130.4 %copy-start.53 = (bf16[192]{0:T(256)(128)(2,1)S(1)}, bf16[192]{0:T(256)(128)(2,1)}, u32[]{:S(2)}) copy-start(bf16[192]{0:T(256)(128)(2,1)} %param.26) | copy-start | bytes 1156
  498.0 55.8 %collective-permute-start = (bf16[768,768]{1,0:T(8,128)(2,1)}, bf16[768,768]{1,0:T(8,128)(2,1)S(1)}, u32[]{:S(2)}, u32[]{:S(2)}) collective-permute-start(bf16[768,768]{1,0:T(8,128)(2,1)} %param.25), channel_id=1, source_target_pairs={{0,1},{1,2},{2,3},{3,0},{4,5},{5,6},{6,7},{7,4},{8,9},{9,10},{10,1... | collective-permute-start | bytes 3538952 | tf_op jit(solution)/shard_map/ppermute | solution.py:21
  554.9 58.4 %collective-permute-start.1 = (bf16[768,768]{1,0:T(8,128)(2,1)S(1)}, bf16[768,768]{1,0:T(8,128)(2,1)}, u32[]{:S(2)}, u32[]{:S(2)}) collective-permute-start(bf16[768,768]{1,0:T(8,128)(2,1)S(1)} %collective-permute-done), channel_id=1, source_target_pairs={{0,1},{1,2},{2,3},{3,0},{4,5},{5,6},{6,7},{7,4},{8,9},{9,10},{10,1... | collective-permute-start | bytes 3538952 | tf_op jit(solution)/shard_map/ppermute | solution.py:21
  613.3 66.2 %collective-permute-start.2 = (bf16[768,768]{1,0:T(8,128)(2,1)}, bf16[768,768]{1,0:T(8,128)(2,1)}, u32[]{:S(2)}, u32[]{:S(2)}) collective-permute-start(bf16[768,768]{1,0:T(8,128)(2,1)} %collective-permute-done.1), channel_id=1, source_target_pairs={{0,1},{1,2},{2,3},{3,0},{4,5},{5,6},{6,7},{7,4},{8,9},{9,10},{10,1... | collective-permute-start | bytes 3538952 | tf_op jit(solution)/shard_map/ppermute | solution.py:21
  631.1 50.7 %copy-start.51 = (bf16[768,2304]{1,0:T(8,128)(2,1)S(1)}, bf16[768,2304]{1,0:T(8,128)(2,1)}, u32[]{:S(2)}) copy-start(bf16[768,2304]{1,0:T(8,128)(2,1)} %all-gather.6.cloned.1.call-done) | copy-start | bytes 10616836
  701.0 43.7 %copy-start.6 = (f32[1024,768]{0,1:T(8,128)S(1)}, f32[1024,768]{0,1:T(8,128)}, u32[]{:S(2)}) copy-start(f32[1024,768]{0,1:T(8,128)} %copy-done.4) | copy-start | bytes 9437188
  (34 other events, 162.1 us)
Sparse Core Ops, SparseCore 0:
  9.6 73.1 all-gather.5
  84.4 28.7 all-gather.7
  114.8 88.5 all-gather.9
  204.8 87.7 all-gather.11
  453.1 27.7 reduce-scatter.6
  483.0 90.1 reduce-scatter.4
  575.5 126.2 reduce-scatter.8
  704.1 84.7 reduce-scatter.10
